TPU v7x, 256 devices: a whole 4x4x8 slice. The times are simulated.
256 devices in a mesh: side: 2 (over x_hi), row: 32 (over y, z), col: 4 (over x_lo, core).
Axes of the slice: x: 4 (x_hi: 2, x_lo: 2; x = x_hi * 2 + x_lo), y: 4, z: 8, core: 2. Of those that a mesh axis runs over, the one named last changes fastest.
Arguments:
- old_vectors: bfloat16 [2, 32768, 16384], P('side', 'row', 'col'), may hold values from -6 to 6
- reflectors: bfloat16 [2, 2, 32768, 512], P('side', None, 'row', 'col'), may hold values from -0.0625 to 0.0625
- triangles: float32 [2, 2, 512, 512], P('side'), may hold values from -0.25 to 0.25
- pole_sq: float32 [32768], replicated, may hold values from 1 to 65536, as said below
- coupling: float32 [32768], replicated, may hold values from -1 to 1
- deflated: int32 [32768], replicated, may hold values 0 or 1
- pole_order: int32 [32768], replicated, may hold values from 0 to 32767, each once
- anchors: int32 [1024], replicated, may hold values from 0 to 32766, as said below
- root_fraction: float32 [1024], replicated, may hold values from 0.2 to 0.8
Outputs:
- vectors: bfloat16 [2, 1024, 32768], P('side', 'col', 'row')
Inputs may be any that keep to these rules, and one draw needn't show every extreme that they name: `pole_sq`: strictly increasing; successive entries differ by 0.5 or more. `anchors`: distinct entries.
All inputs are finite; a program needn't handle non-finite values.
Results may differ from a plain program's by a relative error of at most 0.014.
Values may be sent and summed in bfloat16 or wider, within the bound.
A program may use at most 128 MiB of HBM per device.

v0:
```python
import jax
import jax.numpy as jnp
from jax import lax
from jax.sharding import PartitionSpec as P


def secular_columns(col_sq, col_coupling, col_live, weight, anchor_sq, pole_gap, root_fraction):
    denom = col_sq[:, None] - anchor_sq[None, :] - root_fraction[None, :] * pole_gap[None, :]
    return (col_live * col_coupling * weight)[:, None] / denom


def per_device(
    old_vectors,
    reflectors,
    triangles,
    pole_sq,
    coupling,
    deflated,
    pole_order,
    anchors,
    root_fraction,
):
    side_index = lax.axis_index("side")
    row_index = lax.axis_index("row")
    col_index = lax.axis_index("col")
    half_rows = lax.axis_size("row") // 2
    col_count = lax.axis_size("col")
    old_block = old_vectors[0]
    col_width = old_block.shape[1]
    order_size = pole_sq.shape[0]
    triplets = anchors.shape[0]
    local_triplets = triplets // col_count
    first_column = row_index // half_rows * (order_size // 2) + col_index * col_width
    columns = first_column + jnp.arange(col_width, dtype=jnp.int32)
    position = (
        jnp.zeros((order_size,), jnp.int32)
        .at[pole_order]
        .set(jnp.arange(order_size, dtype=jnp.int32))
    )
    sorted_pos = lax.dynamic_slice_in_dim(position, first_column, col_width)
    col_sq = pole_sq[sorted_pos]
    col_coupling = coupling[sorted_pos]
    col_live = (1 - deflated[sorted_pos]).astype(jnp.float32)
    weight = jnp.where(side_index == 0, jnp.ones_like(col_sq), jnp.sqrt(col_sq))
    anchor_sq = pole_sq[anchors]
    pole_gap = pole_sq[anchors + 1] - anchor_sq
    dead_triplet = deflated[anchors] == 1
    target = pole_order[anchors]
    secular = secular_columns(
        col_sq, col_coupling, col_live, weight, anchor_sq, pole_gap, root_fraction
    )
    onehot = (columns[:, None] == target[None, :]).astype(jnp.float32)
    mixing = jnp.where(dead_triplet[None, :], onehot, secular).astype(jnp.bfloat16)
    share_size = col_width // half_rows
    slice_part = lax.dynamic_slice_in_dim(
        secular, row_index % half_rows * share_size, share_size, 0
    )
    squares = lax.psum(jnp.sum(slice_part * slice_part, axis=0), ("row", "col"))
    col_scale = jnp.where(dead_triplet, jnp.ones_like(squares), 1.0 / jnp.sqrt(squares + 1e-06))
    merged = lax.psum_scatter(
        jnp.einsum("ck,rc->kr", mixing, old_block, preferred_element_type=jnp.float32).astype(
            jnp.bfloat16
        ),
        "col",
        scatter_dimension=0,
        tiled=True,
    ).astype(jnp.float32)
    my_scale = lax.dynamic_slice_in_dim(col_scale, col_index * local_triplets, local_triplets)
    vectors = merged * my_scale[:, None]
    panel_local = reflectors[0]
    panels = panel_local.shape[0]
    upper_tri = jnp.triu(triangles[0])
    highest = lax.Precision.HIGHEST
    for panel_index in reversed(range(panels)):
        panel_rows = panel_local[panel_index]
        current = vectors
        current_low = current.astype(jnp.bfloat16)
        projected = jnp.dot(
            current_low,
            lax.all_gather(panel_rows, "col", axis=1, tiled=True),
            preferred_element_type=jnp.float32,
        )
        projected = lax.psum(projected.astype(jnp.bfloat16), "row").astype(jnp.float32)
        coefficients = jnp.dot(projected, upper_tri[panel_index].T, precision=highest).astype(
            jnp.bfloat16
        )
        vectors = current - jnp.dot(
            coefficients,
            lax.all_gather(panel_rows, "col", axis=1, tiled=True).T,
            preferred_element_type=jnp.float32,
        )
    return vectors.astype(jnp.bfloat16)[None]


def solution(mesh):
    in_specs = (
        P("side", "row", "col"),
        P("side", None, "row", "col"),
        P("side", None, None, None),
        P(),
        P(),
        P(),
        P(),
        P(),
        P(),
    )
    out_specs = P("side", "col", "row")
    return jax.shard_map(
        per_device, mesh=mesh, in_specs=in_specs, out_specs=out_specs, check_vma=False
    )
```

profile of v0, /device:TPU:2, one launch (start us, length us, event | category | flops | bytes accessed | tf_op | source)
XLA Modules:
  0.0 883.1 jit_solution(16158088718118967877)
XLA Ops:
  6.5 1.9 fusion.23
  8.4 0.0 reduce-scatter.2.cloned.1.call-start
  8.5 0.9 compare_select_fusion
  9.5 120.1 %scatter_custom_fusion = s32[32768]{0:T(1024)S(1)} fusion(s32[32768]{0:T(1024)S(1)} %compare_select_fusion, s32[32768]{0:T(1024)S(1)} %iota.24, s32[]{:T(128)} %constant.23.clone.1), kind=kCustom, calls=%fused_computation.38 | custom fusion | bytes 131076 | tf_op jit(solution)/shard_map/scatter | solution.py:38
  129.6 19.5 %gather_fusion.2 = s32[4096]{0:T(1024)S(1)} fusion(s32[32768]{0:T(1024)} %param.14, s32[4096]{0:T(1024)S(1)} %fusion.20), kind=kCustom, calls=%fused_computation.2 | custom fusion | bytes 49152 | tf_op jit(solution)/shard_map/gather | solution.py:43
  149.2 23.0 %gather_fusion.4 = f32[4096]{0:T(1024)S(1)} fusion(f32[32768]{0:T(1024)S(1)} %copy-done, s32[4096]{0:T(1024)S(1)} %fusion.20), kind=kCustom, calls=%fused_computation.4 | custom fusion | bytes 49152 | tf_op jit(solution)/shard_map/gather | solution.py:41
  172.3 6.2 gather_fusion.5
  178.4 6.2 gather_fusion
  184.6 6.2 gather_fusion.1
  190.8 23.0 %gather_fusion.3 = f32[4096]{0:T(1024)S(1)} fusion(f32[32768]{0:T(1024)S(1)} %copy-done.2, s32[4096]{0:T(1024)S(1)} %fusion.20), kind=kCustom, calls=%fused_computation.3 | custom fusion | bytes 49152 | tf_op jit(solution)/shard_map/gather | solution.py:42
  213.8 6.2 gather_fusion.6
  220.0 6.5 subtract_divide_fusion
  226.5 1.3 multiply_reduce_fusion
  227.8 278.5 %psum.21 = f32[1024]{0:T(1024)S(1)} all-reduce(f32[1024]{0:T(1024)S(1)} %multiply_reduce_fusion), channel_id=1, replica_groups=mesh['side'=2,'row'=32,'col'=4] {'row','col'}, use_global_device_ids=true, to_apply=%region_3.4 | all-reduce | flops 1024 | bytes 8192 | tf_op jit(solution)/shard_map/psum | solution.py:58
  506.3 15.3 %fusion.5 = bf16[1024,1024]{1,0:T(8,128)(2,1)} fusion(bf16[1,1024,4096]{2,1,0:T(8,128)(2,1)} %param.9, s32[1024]{0:T(1024)S(1)} %gather_fusion.1, s32[4096]{0:T(1024)S(1)} %iota_add_fusion, pred[1024]{0:T(1024)(128)(4,1)S(1)} %get-tuple-element.6, f32[1024]{0:T(1024)S(1)} %subtract_multiply_fusion, f32[1024]{0:T(1024)S(1)} %gather_fusion.5, ...), kind=kOutput, calls=%fused_computation.16 | convolution fusion | flops 8620343296 | bytes 10548224 | tf_op jit(solution)/shard_map/ck,rc->kr/dot_general | solution.py:61
  521.7 0.0 all-reduce.3.cloned.1.call-start
  521.8 0.1 dynamic_slice.11
  521.8 28.4 %reduce-scatter.2.cloned.1.call-done = bf16[256,1024]{1,0:T(8,128)(2,1)} async-done(((bf16[1024,1024]{1,0:T(8,128)(2,1)}), bf16[256,1024]{1,0:T(8,128)(2,1)}) %reduce-scatter.2.cloned.1.call-update) | async-done | bytes 524304 | tf_op jit(solution)/shard_map/reduce_scatter | solution.py:60
  550.3 2.6 convolution_convert_fusion.3
  552.9 0.0 all-gather.7.cloned.1.call-start
  552.9 0.5 all-gather.7.cloned.1.call-update
  553.5 0.3 all-reduce.5.cloned.1.call-start
  553.7 0.2 iota_compare_fusion
  554.0 2.0 bitcast_select_fusion
  555.9 145.1 %all-reduce.3.cloned.1.call-done = bf16[256,512]{1,0:T(8,128)(2,1)} async-done(((bf16[256,512]{1,0:T(8,128)(2,1)}), bf16[256,512]{1,0:T(8,128)(2,1)}) %all-reduce.3.cloned.1.call-update) | async-done | bytes 262160 | tf_op jit(solution)/shard_map/psum | solution.py:83
  701.0 1.6 convolution_convert_fusion.2
  702.6 1.8 convolution_subtract_fusion.1
  704.5 18.7 %all-gather.7.cloned.1.call-done = bf16[1,1,1024,512]{3,2,1,0:T(8,128)(2,1)} async-done(((bf16[1,1,1024,128]{3,2,1,0:T(8,128)(2,1)}), bf16[1,1,1024,512]{3,2,1,0:T(8,128)(2,1)}) %all-gather.7.cloned.1.call-update) | async-done | bytes 1048592 | tf_op jit(solution)/shard_map/all_gather | solution.py:80
  723.1 2.4 convolution_convert_fusion.1
  725.5 146.9 %all-reduce.5.cloned.1.call-done = bf16[256,512]{1,0:T(8,128)(2,1)} async-done(((bf16[256,512]{1,0:T(8,128)(2,1)}), bf16[256,512]{1,0:T(8,128)(2,1)}) %all-reduce.5.cloned.1.call-update) | async-done | bytes 262160 | tf_op jit(solution)/shard_map/psum | solution.py:83
  872.4 1.6 convolution_convert_fusion
  874.1 2.5 fusion.9
  (26 shorter events, 0.2 us)
Async XLA Ops:
  6.5 142.6 %copy-start = (f32[32768]{0:T(1024)S(1)}, f32[32768]{0:T(1024)}, u32[]{:S(2)}) copy-start(f32[32768]{0:T(1024)} %param.12) | copy-start | bytes 393220
  6.5 515.3 %all-gather.5.cloned.1.call-start = ((), (), s32[]{:S(2)}) async-start(), calls=%async_computation.4 | async-start | bytes 1310720 | tf_op jit(solution)/shard_map/all_gather | solution.py:80
  8.4 541.8 %reduce-scatter.2.cloned.1.call-start = ((), (), s32[]{:S(2)}) async-start(), calls=%async_computation.1 | async-start | bytes 2621440 | tf_op jit(solution)/shard_map/reduce_scatter | solution.py:60
  129.6 42.6 %copy-start.4 = (s32[1024]{0:T(1024)S(1)}, s32[1024]{0:T(1024)}, u32[]{:S(2)}) copy-start(s32[1024]{0:T(1024)} %param.16) | copy-start | bytes 12292
  129.6 48.8 %copy-start.1 = (s32[32768]{0:T(1024)S(1)}, s32[32768]{0:T(1024)}, u32[]{:S(2)}) copy-start(s32[32768]{0:T(1024)} %param.14) | copy-start | bytes 393220
  149.2 35.4 %copy-start.3 = (s32[32768]{0:T(1024)S(1)}, s32[32768]{0:T(1024)}, u32[]{:S(2)}) copy-start(s32[32768]{0:T(1024)} %param.15) | copy-start | bytes 393220
  149.2 41.6 %copy-start.2 = (f32[32768]{0:T(1024)S(1)}, f32[32768]{0:T(1024)}, u32[]{:S(2)}) copy-start(f32[32768]{0:T(1024)} %param.13) | copy-start | bytes 393220
  172.3 47.7 %copy-start.5 = (f32[1024]{0:T(1024)S(1)}, f32[1024]{0:T(1024)}, u32[]{:S(2)}) copy-start(f32[1024]{0:T(1024)} %param.17) | copy-start | bytes 12292
  521.7 179.3 %all-reduce.3.cloned.1.call-start = ((), (), s32[]{:S(2)}) async-start(), calls=%async_computation.2 | async-start | bytes 524288 | tf_op jit(solution)/shard_map/psum | solution.py:83
  552.9 170.3 %all-gather.7.cloned.1.call-start = ((), (), s32[]{:S(2)}) async-start(), calls=%async_computation.5 | async-start | bytes 1310720 | tf_op jit(solution)/shard_map/all_gather | solution.py:80
  553.5 319.0 %all-reduce.5.cloned.1.call-start = ((), (), s32[]{:S(2)}) async-start(), calls=%async_computation.3 | async-start | bytes 524288 | tf_op jit(solution)/shard_map/psum | solution.py:83
Sparse Core Ops, SparseCore 0:
  9.2 26.2 all-gather.4
  521.8 28.4 reduce-scatter.1
  554.1 146.8 all-reduce.2
  702.8 20.2 all-gather.6
  726.8 145.5 all-reduce.4
where the time goes:
time: 884 us; the launch traced here: 883 us
  waiting for transfers between devices  340 us (38%)
  blocking collectives  278 us (31%)
  local copies, waits for them, and re-layouts  212 us (24%)
  matrix products  27.8 us (3%)
  between operations  13.4 us (2%)
  other arithmetic  10.9 us (1%)
    psum x2, waiting for transfers between devices, per_device(): lax.psum(projected.astype(jnp.bfloat16), 'row').astype(jnp.float32)  292 us
    psum x1, blocking collectives, per_device(): squares = lax.psum(jnp.sum(slice_part * slice_part, axis=0), ('row', 'col'))  278 us
    scatter x1, local copies, waits for them, and re-layouts, per_device(): position = jnp.zeros((order_size,), jnp.int32).at[pole_order].set(jnp.ara...  120 us
    reduce_scatter x1, waiting for transfers between devices, per_device(): lax.psum_scatter(jnp.einsum('ck,rc->kr', mixing, old_block, preferred_ele...  28.4 us
    gather x1, local copies, waits for them, and re-layouts, per_device(): col_sq = pole_sq[sorted_pos]  23 us
    gather x1, local copies, waits for them, and re-layouts, per_device(): col_coupling = coupling[sorted_pos]  23 us
    gather x1, local copies, waits for them, and re-layouts, per_device(): col_live = (1 - deflated[sorted_pos]).astype(jnp.float32)  19.5 us
    all_gather x2, waiting for transfers between devices, per_device(): lax.all_gather(panel_rows, 'col', axis=1, tiled=True)  18.7 us
  transfers between devices with their start and end apart: 5, of which 4 were waited for; matrix products, arithmetic and copies ran while one was open for 27% of the time, Pallas kernels for 0%

commit v1 on v0

--- a/solution.py
+++ b/solution.py
@@ -55,7 +55,9 @@
     slice_part = lax.dynamic_slice_in_dim(
         secular, row_index % half_rows * share_size, share_size, 0
     )
-    squares = lax.psum(jnp.sum(slice_part * slice_part, axis=0), ("row", "col"))
+    squares = jnp.sum(slice_part * slice_part, axis=0)
+    for over in ("row", "col"):
+        squares = lax.psum(squares, over)
     col_scale = jnp.where(dead_triplet, jnp.ones_like(squares), 1.0 / jnp.sqrt(squares + 1e-06))
     merged = lax.psum_scatter(
         jnp.einsum("ck,rc->kr", mixing, old_block, preferred_element_type=jnp.float32).astype(

time: 884 us -> 683 us (0.77)
  blocking collectives: 278 us -> 83.8 us
    psum x1 -> x2, blocking collectives: 278 us -> 83.8 us  [per_device(): squares = lax.psum(squares, over)]
  transfers between devices with their start and end apart: 5 -> 5, of which waited for: 4 -> 4; matrix products, arithmetic and copies ran while one was open for 27% -> 35% of each run, Pallas kernels for 0% -> 0%
where the time goes in v1:
time: 683 us; the launch traced here: 682 us
  waiting for transfers between devices  334 us (49%)
  local copies, waits for them, and re-layouts  212 us (31%)
  blocking collectives  83.8 us (12%)
  matrix products  27.8 us (4%)
  between operations  13.4 us (2%)
  other arithmetic  10.9 us (2%)
    psum x2, waiting for transfers between devices, per_device(): lax.psum(projected.astype(jnp.bfloat16), 'row').astype(jnp.float32)  292 us
    scatter x1, local copies, waits for them, and re-layouts, per_device(): position = jnp.zeros((order_size,), jnp.int32).at[pole_order].set(jnp.ara...  120 us
    psum x2, blocking collectives, per_device(): squares = lax.psum(squares, over)  83.8 us
    gather x1, local copies, waits for them, and re-layouts, per_device(): col_sq = pole_sq[sorted_pos]  23 us
    gather x1, local copies, waits for them, and re-layouts, per_device(): col_coupling = coupling[sorted_pos]  23 us
    reduce_scatter x1, waiting for transfers between devices, per_device(): lax.psum_scatter(jnp.einsum('ck,rc->kr', mixing, old_block, preferred_ele...  22.6 us
    gather x1, local copies, waits for them, and re-layouts, per_device(): col_live = (1 - deflated[sorted_pos]).astype(jnp.float32)  19.5 us
    all_gather x2, waiting for transfers between devices, per_device(): lax.all_gather(panel_rows, 'col', axis=1, tiled=True)  18.7 us
  transfers between devices with their start and end apart: 5, of which 4 were waited for; matrix products, arithmetic and copies ran while one was open for 35% of the time, Pallas kernels for 0%

profile of v1, /device:TPU:2, one launch (start us, length us, event | category | flops | bytes accessed | tf_op | source)
XLA Modules:
  0.0 682.5 jit_solution(9622185338462220297)
XLA Ops:
  6.5 1.9 fusion.23
  8.4 0.0 reduce-scatter.2.cloned.1.call-start
  8.5 0.9 compare_select_fusion
  9.5 120.1 %scatter_custom_fusion = s32[32768]{0:T(1024)S(1)} fusion(s32[32768]{0:T(1024)S(1)} %compare_select_fusion, s32[32768]{0:T(1024)S(1)} %iota.24, s32[]{:T(128)} %constant.23.clone.1), kind=kCustom, calls=%fused_computation.38 | custom fusion | bytes 131076 | tf_op jit(solution)/shard_map/scatter | solution.py:38
  129.6 19.5 %gather_fusion.2 = s32[4096]{0:T(1024)S(1)} fusion(s32[32768]{0:T(1024)} %param.14, s32[4096]{0:T(1024)S(1)} %fusion.20), kind=kCustom, calls=%fused_computation.2 | custom fusion | bytes 49152 | tf_op jit(solution)/shard_map/gather | solution.py:43
  149.2 23.0 %gather_fusion.4 = f32[4096]{0:T(1024)S(1)} fusion(f32[32768]{0:T(1024)S(1)} %copy-done, s32[4096]{0:T(1024)S(1)} %fusion.20), kind=kCustom, calls=%fused_computation.4 | custom fusion | bytes 49152 | tf_op jit(solution)/shard_map/gather | solution.py:41
  172.3 6.2 gather_fusion.5
  178.4 6.2 gather_fusion
  184.6 6.2 gather_fusion.1
  190.8 23.0 %gather_fusion.3 = f32[4096]{0:T(1024)S(1)} fusion(f32[32768]{0:T(1024)S(1)} %copy-done.2, s32[4096]{0:T(1024)S(1)} %fusion.20), kind=kCustom, calls=%fused_computation.3 | custom fusion | bytes 49152 | tf_op jit(solution)/shard_map/gather | solution.py:42
  213.8 6.2 gather_fusion.6
  220.0 6.4 subtract_divide_fusion
  226.5 1.3 multiply_reduce_fusion
  227.8 77.9 %psum.28 = f32[1024]{0:T(1024)S(1)} all-reduce(f32[1024]{0:T(1024)S(1)} %multiply_reduce_fusion), channel_id=1, replica_groups=mesh['side'=2,'row'=32,'col'=4] {'row'}, use_global_device_ids=true, to_apply=%region_3.4 | all-reduce | flops 1024 | bytes 8192 | tf_op jit(solution)/shard_map/psum | solution.py:60
  305.7 5.9 psum.29
  311.7 15.3 %fusion.5 = bf16[1024,1024]{1,0:T(8,128)(2,1)} fusion(bf16[1,1024,4096]{2,1,0:T(8,128)(2,1)} %param.9, s32[1024]{0:T(1024)S(1)} %gather_fusion.1, s32[4096]{0:T(1024)S(1)} %iota_add_fusion, pred[1024]{0:T(1024)(128)(4,1)S(1)} %get-tuple-element.6, f32[1024]{0:T(1024)S(1)} %subtract_multiply_fusion, f32[1024]{0:T(1024)S(1)} %gather_fusion.5, ...), kind=kOutput, calls=%fused_computation.16 | convolution fusion | flops 8620343296 | bytes 10548224 | tf_op jit(solution)/shard_map/ck,rc->kr/dot_general | solution.py:63
  327.0 0.0 all-reduce.3.cloned.1.call-start
  327.1 0.1 dynamic_slice.11
  327.1 22.6 %reduce-scatter.2.cloned.1.call-done = bf16[256,1024]{1,0:T(8,128)(2,1)} async-done(((bf16[1024,1024]{1,0:T(8,128)(2,1)}), bf16[256,1024]{1,0:T(8,128)(2,1)}) %reduce-scatter.2.cloned.1.call-update) | async-done | bytes 524304 | tf_op jit(solution)/shard_map/reduce_scatter | solution.py:62
  349.7 2.6 convolution_convert_fusion.3
  352.4 0.5 all-gather.7.cloned.1.call-update
  352.9 0.3 all-reduce.5.cloned.1.call-start
  353.2 0.2 iota_compare_fusion
  353.4 2.0 bitcast_select_fusion
  355.3 145.0 %all-reduce.3.cloned.1.call-done = bf16[256,512]{1,0:T(8,128)(2,1)} async-done(((bf16[256,512]{1,0:T(8,128)(2,1)}), bf16[256,512]{1,0:T(8,128)(2,1)}) %all-reduce.3.cloned.1.call-update) | async-done | bytes 262160 | tf_op jit(solution)/shard_map/psum | solution.py:85
  500.4 1.6 convolution_convert_fusion.2
  502.0 1.8 convolution_subtract_fusion.1
  503.9 18.7 %all-gather.7.cloned.1.call-done = bf16[1,1,1024,512]{3,2,1,0:T(8,128)(2,1)} async-done(((bf16[1,1,1024,128]{3,2,1,0:T(8,128)(2,1)}), bf16[1,1,1024,512]{3,2,1,0:T(8,128)(2,1)}) %all-gather.7.cloned.1.call-update) | async-done | bytes 1048592 | tf_op jit(solution)/shard_map/all_gather | solution.py:82
  522.5 2.4 convolution_convert_fusion.1
  524.9 146.9 %all-reduce.5.cloned.1.call-done = bf16[256,512]{1,0:T(8,128)(2,1)} async-done(((bf16[256,512]{1,0:T(8,128)(2,1)}), bf16[256,512]{1,0:T(8,128)(2,1)}) %all-reduce.5.cloned.1.call-update) | async-done | bytes 262160 | tf_op jit(solution)/shard_map/psum | solution.py:85
  671.8 1.6 convolution_convert_fusion
  673.4 2.5 fusion.9
  (27 shorter events, 0.2 us)
Async XLA Ops:
  6.5 142.6 %copy-start = (f32[32768]{0:T(1024)S(1)}, f32[32768]{0:T(1024)}, u32[]{:S(2)}) copy-start(f32[32768]{0:T(1024)} %param.12) | copy-start | bytes 393220
  6.5 320.6 %all-gather.5.cloned.1.call-start = ((), (), s32[]{:S(2)}) async-start(), calls=%async_computation.4 | async-start | bytes 1310720 | tf_op jit(solution)/shard_map/all_gather | solution.py:82
  8.4 341.2 %reduce-scatter.2.cloned.1.call-start = ((), (), s32[]{:S(2)}) async-start(), calls=%async_computation.1 | async-start | bytes 2621440 | tf_op jit(solution)/shard_map/reduce_scatter | solution.py:62
  129.6 42.6 %copy-start.4 = (s32[1024]{0:T(1024)S(1)}, s32[1024]{0:T(1024)}, u32[]{:S(2)}) copy-start(s32[1024]{0:T(1024)} %param.16) | copy-start | bytes 12292
  129.6 48.8 %copy-start.1 = (s32[32768]{0:T(1024)S(1)}, s32[32768]{0:T(1024)}, u32[]{:S(2)}) copy-start(s32[32768]{0:T(1024)} %param.14) | copy-start | bytes 393220
  149.2 35.4 %copy-start.3 = (s32[32768]{0:T(1024)S(1)}, s32[32768]{0:T(1024)}, u32[]{:S(2)}) copy-start(s32[32768]{0:T(1024)} %param.15) | copy-start | bytes 393220
  149.2 41.6 %copy-start.2 = (f32[32768]{0:T(1024)S(1)}, f32[32768]{0:T(1024)}, u32[]{:S(2)}) copy-start(f32[32768]{0:T(1024)} %param.13) | copy-start | bytes 393220
  172.3 47.7 %copy-start.5 = (f32[1024]{0:T(1024)S(1)}, f32[1024]{0:T(1024)}, u32[]{:S(2)}) copy-start(f32[1024]{0:T(1024)} %param.17) | copy-start | bytes 12292
  327.0 173.4 %all-reduce.3.cloned.1.call-start = ((), (), s32[]{:S(2)}) async-start(), calls=%async_computation.2 | async-start | bytes 524288 | tf_op jit(solution)/shard_map/psum | solution.py:85
  352.3 170.2 %all-gather.7.cloned.1.call-start = ((), (), s32[]{:S(2)}) async-start(), calls=%async_computation.5 | async-start | bytes 1310720 | tf_op jit(solution)/shard_map/all_gather | solution.py:82
  352.9 318.9 %all-reduce.5.cloned.1.call-start = ((), (), s32[]{:S(2)}) async-start(), calls=%async_computation.3 | async-start | bytes 524288 | tf_op jit(solution)/shard_map/psum | solution.py:85
Sparse Core Ops, SparseCore 0:
  9.2 26.2 all-gather.4
  327.1 22.5 reduce-scatter.1
  353.6 146.7 all-reduce.2
  502.2 20.2 all-gather.6
  526.2 145.5 all-reduce.4
